TPU v7x, 1024 devices: a whole 8x8x8 slice. The times are simulated.
1024 devices in a mesh: ctx: 128 (over y, z, core), head: 8 (over x).
Axes of the slice: x: 8, y: 8, z: 8, core: 2. Of those that a mesh axis runs over, the one named last changes fastest.
Arguments:
- query: bfloat16 [16384, 4096], P('ctx', 'head'), may hold values from -6 to 6
- keys: bfloat16 [16384, 4096], P('ctx', 'head'), may hold values from -10 to 10
- values: bfloat16 [16384, 4096], P('ctx', 'head'), may hold values from -12 to 12
- log_decay: float32 [16384, 32], P('ctx', 'head'), may hold values from -1 to 0
- norm_gain: float32 [4096], P('head'), may hold values from 0.1 to 1.9
- out_weight: bfloat16 [4096, 6144], P('head'), may hold values from -0.125 to 0.125
Outputs:
- mixed: bfloat16 [16384, 6144], P('ctx', 'head')
All inputs are finite; a program needn't handle non-finite values.
Results may differ from a plain program's by a relative error of at most 0.014.
Values may be sent and summed in bfloat16 or wider, within the bound.
A program may use at most 128 MiB of HBM per device.

v0:
```python
import jax
import jax.numpy as jnp
from jax import lax
from jax.sharding import PartitionSpec as P


def entering(value, axis, join, neutral):
    count, mine = (lax.axis_size(axis), lax.axis_index(axis))
    pieces = jax.tree.map(lambda part: lax.all_gather(part, axis), value)
    so_far = jax.tree.map(
        lambda part, zero: jnp.full_like(part, 0) + jnp.asarray(zero, part.dtype), value, neutral
    )

    def hop(position, so_far):
        longer = join(so_far, jax.tree.map(lambda part: part[position], pieces))
        return jax.tree.map(lambda new, old: jnp.where(position < mine, new, old), longer, so_far)

    return lax.fori_loop(0, count - 1, hop, so_far)


def combine_states(earlier, later):
    return (earlier[0] * later[0], later[0][:, None, None] * earlier[1] + later[1])


def local(query, keys, values, log_decay, norm_gain, out_weight):
    tok_rows, full_width = query.shape
    head_count = log_decay.shape[1]
    head_dim = full_width // head_count

    def by_head(array):
        return array.reshape(tok_rows, head_count, head_dim).transpose(1, 0, 2)

    queries = by_head(query)
    key_rows = by_head(keys)
    value_rows = by_head(values)
    cumulative = jnp.cumsum(log_decay.T, axis=1)
    tail_decay = jnp.exp(cumulative[:, -1:] - cumulative)
    kv_local = jnp.einsum(
        "hte,htf->hef",
        key_rows.astype(jnp.float32) * tail_decay[:, :, None],
        value_rows.astype(jnp.float32),
        precision=lax.Precision.HIGHEST,
    )
    decay_total = jnp.exp(cumulative[:, -1])
    carried = entering(
        (decay_total, kv_local),
        "ctx",
        combine_states,
        (jnp.ones_like(decay_total), jnp.zeros_like(kv_local)),
    )
    state_in = carried[1]
    row_index = lax.broadcasted_iota(jnp.int32, (tok_rows, tok_rows), 0)
    col_index = lax.broadcasted_iota(jnp.int32, (tok_rows, tok_rows), 1)
    causal = (row_index >= col_index)[None]
    scores = jnp.einsum("hte,hse->hts", queries, key_rows, preferred_element_type=jnp.float32)
    differ = jnp.where(causal, cumulative[:, :, None] - cumulative[:, None, :], -1e30)
    block_weights = (jnp.exp(differ) * scores).astype(jnp.bfloat16)
    within = jnp.einsum(
        "hts,hse->hte", block_weights, value_rows, preferred_element_type=jnp.float32
    )
    carried_part = jnp.exp(cumulative)[:, :, None] * jnp.einsum(
        "hte,hef->htf", queries.astype(jnp.float32), state_in, precision=lax.Precision.HIGHEST
    )
    attn = (within + carried_part).transpose(1, 0, 2).reshape(tok_rows, full_width)
    squares = lax.psum(jnp.sum(attn * attn, axis=1), "head")
    row_scale = lax.rsqrt(squares / (full_width * lax.axis_size("head")) + 1e-05)
    normed = (attn * row_scale[:, None] * norm_gain[None, :]).astype(jnp.bfloat16)
    partial_out = jnp.dot(normed, out_weight, preferred_element_type=jnp.float32)
    mixed = lax.psum_scatter(
        partial_out.astype(jnp.bfloat16), "head", scatter_dimension=1, tiled=True
    )
    return mixed


def solution(mesh):
    placed = (
        P("ctx", "head"),
        P("ctx", "head"),
        P("ctx", "head"),
        P("ctx", "head"),
        P("head"),
        P("head", None),
    )
    return jax.shard_map(
        local, mesh=mesh, in_specs=placed, out_specs=P("ctx", "head"), check_vma=False
    )
```

profile of v0, /device:TPU:2, one launch (start us, length us, event | category | flops | bytes accessed | tf_op | source)
XLA Modules:
  0.0 488.3 jit_solution(9124994055737690784)
XLA Ops:
  8.9 1.9 fusion.6
  10.8 1.3 dynamic-slice
  13.0 269.8 %all-reduce = f32[512]{0:T(512)S(1)} all-reduce(f32[512]{0:T(512)S(1)} %dynamic-update-slice), channel_id=2, replica_groups=mesh['ctx'=128,'head'=8] {'ctx'}, use_global_device_ids=true, to_apply=%add | all-reduce | flops 512 | bytes 4096
  283.0 1.3 convolution_bitcast_fusion.1
  284.3 138.9 %while.14 = (s32[]{:T(128)}, f32[4,128,128]{2,1,0:T(8,128)S(1)}, s32[]{:T(128)}, f32[128,4]{1,0:T(8,128)S(1)}, f32[128,4,128,128]{3,2,1,0:T(8,128)}, /*index=5*/s32[]{:T(128)}, s32[]{:T(128)}) while((s32[]{:T(128)}, f32[4,128,128]{2,1,0:T(8,128)S(1)}, s32[]{:T(128)}, f32[128,4]{1,0:T(8,128)S(1)}, f32[128,4,128,128]{3,2,1,0:T(8,128)}, ...), condition=%wide.region_2.3_spmd.clone, body=%wide.region_1.2_spmd.clone.sunk | while | flops 262148 | bytes 786585 | solution.py:18
  284.3 1.1 fusion.32
  285.4 1.1 fusion.32
  288.7 1.1 fusion.32
  289.8 1.1 fusion.32
  290.9 1.1 fusion.32
  294.2 1.1 fusion.32
  295.3 1.1 fusion.32
  298.6 1.1 fusion.32
  299.6 1.1 fusion.32
  300.7 1.1 fusion.32
  304.0 1.1 fusion.32
  305.1 1.1 fusion.32
  306.2 1.1 fusion.32
  309.5 1.1 fusion.32
  310.6 1.1 fusion.32
  311.7 1.1 fusion.32
  315.0 1.1 fusion.32
  316.0 1.1 fusion.32
  319.3 1.1 fusion.32
  320.4 1.1 fusion.32
  321.5 1.1 fusion.32
  324.8 1.1 fusion.32
  325.9 1.1 fusion.32
  327.0 1.1 fusion.32
  330.3 1.1 fusion.32
  331.4 1.1 fusion.32
  332.5 1.1 fusion.32
  335.7 1.1 fusion.32
  336.8 1.1 fusion.32
  340.1 1.1 fusion.32
  341.2 1.1 fusion.32
  342.3 1.1 fusion.32
  345.6 1.1 fusion.32
  346.7 1.1 fusion.32
  347.8 1.1 fusion.32
  351.0 1.1 fusion.32
  352.1 1.1 fusion.32
  353.2 1.1 fusion.32
  356.5 1.1 fusion.32
  357.6 1.1 fusion.32
  423.6 15.8 %psum.7 = f32[128]{0:T(128)S(1)} all-reduce(f32[128]{0:T(128)S(1)} %get-tuple-element.132), channel_id=1, replica_groups=mesh['ctx'=128,'head'=8] {'head'}, use_global_device_ids=true, to_apply=%region_4.5 | all-reduce | flops 128 | bytes 1024 | tf_op jit(solution)/shard_map/psum | solution.py:65
  439.6 5.0 %convolution_convert_fusion = bf16[128,6144]{1,0:T(8,128)(2,1)} fusion(bf16[128,512]{0,1:T(8,128)(2,1)S(1)} %fusion.5, bf16[512,6144]{1,0:T(8,128)(2,1)} %param.13), kind=kOutput, calls=%fused_computation.3 | convolution fusion | flops 806092800 | bytes 7995392 | tf_op jit(solution)/shard_map/dot_general | solution.py:68
  444.6 36.9 %reduce-scatter.2.cloned.1.call-done = bf16[128,768]{1,0:T(8,128)(2,1)} async-done(((bf16[128,6144]{1,0:T(8,128)(2,1)}), bf16[128,768]{1,0:T(8,128)(2,1)}) %reduce-scatter.2.cloned.1.call-update) | async-done | bytes 196624 | tf_op jit(solution)/shard_map/reduce_scatter | solution.py:69
  (235 shorter events, 96.1 us)
Async XLA Ops:
  6.5 276.5 %copy-start = (bf16[128,512]{1,0:T(8,128)(2,1)S(1)}, bf16[128,512]{1,0:T(8,128)(2,1)}, u32[]{:S(2)}) copy-start(bf16[128,512]{1,0:T(8,128)(2,1)} %param.8) | copy-start | bytes 393220
  6.5 432.9 %copy-start.1 = (f32[512]{0:T(512)S(1)}, f32[512]{0:T(512)}, u32[]{:S(2)}) copy-start(f32[512]{0:T(512)} %param.12) | copy-start | bytes 6148
  6.5 277.7 %all-gather.4.cloned.1.call-start = ((), (), s32[]{:S(2)}) async-start(), calls=%async_computation.2 | async-start | bytes 33816576 | tf_op jit(solution)/shard_map/all_gather | solution.py:9
  10.8 470.7 %reduce-scatter.2.cloned.1.call-start = ((), (), s32[]{:S(2)}) async-start(), calls=%async_computation.1 | async-start | bytes 1769472 | tf_op jit(solution)/shard_map/reduce_scatter | solution.py:69
Sparse Core Ops, SparseCore 0:
  11.6 160.4 all-gather.3
  444.7 36.6 reduce-scatter.1
where the time goes:
time: 493 us; the launch traced here: 488 us
  blocking collectives  286 us (58%)
  other arithmetic  135 us (27%)
  waiting for transfers between devices  36.9 us (7%)
  between operations  14.1 us (3%)
  matrix products  8.52 us (2%)
    unnamed x1, blocking collectives  270 us
    select_n x127, other arithmetic, hop(): jnp.where(position < mine, new, old)  134 us
    reduce_scatter x1, waiting for transfers between devices, local(): lax.psum_scatter(partial_out.astype(jnp.bfloat16), 'head', scatter_dimens...  36.9 us
    psum x1, blocking collectives, local(): squares = lax.psum(jnp.sum(attn * attn, axis=1), 'head')  15.8 us
  transfers between devices with their start and end apart: 2, of which 1 were waited for; matrix products, arithmetic and copies ran while one was open for 1% of the time, Pallas kernels for 0%

commit v1 on v0

v1 whole, which is shorter than its diff:
```python
import functools

import jax
import jax.numpy as jnp
from jax import lax
from jax.experimental import pallas as pl
from jax.experimental.pallas import tpu as pltpu
from jax.sharding import PartitionSpec as P

MESH = pl.DeviceIdType.MESH
HIGHEST = lax.Precision.HIGHEST
LANE = 128
ROW_GROUP = 16
F32 = jnp.float32
BF16 = jnp.bfloat16


def body(
    dims,
    q_hbm, k_hbm, v_hbm, ld_hbm, gain_hbm, w_hbm,
    out_ref,
    q, k, v, ld, gain, w,
    cc, within, act,
    d_send, d_recv, s_send, z_recv, e_buf, pd_buf,
    yd_send, yd_recv, r_send, y_recv, p_send, s_in,
    sq_send, sq_recv, own, tx, rx,
    in_sem, w_sem, d_sem, z_sem, yd_sem, y_send_sem, y_recv_sem, p_sem, sq_sem,
    tx_sem, rx_sem,
):
    nx, ny, group, heads, chunks = dims
    x = lax.axis_index("head")
    ctx = lax.axis_index("ctx")
    y = ctx // group
    j = lax.rem(ctx, group)
    base = y * group
    rows = s_send.shape[1]
    half_x = nx // 2
    half_c = chunks // 2
    width = chunks * LANE
    per_head = LANE // rows

    barrier = pltpu.get_barrier_semaphore()

    def greet_row(r, _):
        pl.semaphore_signal(
            barrier, inc=1, device_id={"ctx": base + lax.rem(j + r, group)}, device_id_type=MESH
        )
        return 0

    def greet_y(r, _):
        pl.semaphore_signal(
            barrier, inc=1, device_id={"ctx": lax.rem(y + r, ny) * group + j}, device_id_type=MESH
        )
        return 0

    def greet_x(r, _):
        pl.semaphore_signal(
            barrier, inc=1, device_id={"head": lax.rem(x + r, nx)}, device_id_type=MESH
        )
        return 0

    ld_in = pltpu.make_async_copy(ld_hbm, ld, in_sem.at[0])
    k_in = pltpu.make_async_copy(k_hbm, k, in_sem.at[1])
    v_in = pltpu.make_async_copy(v_hbm, v, in_sem.at[2])
    q_in = pltpu.make_async_copy(q_hbm, q, in_sem.at[3])
    gain_in = pltpu.make_async_copy(gain_hbm, gain, in_sem.at[4])
    for copy in (ld_in, k_in, v_in, q_in, gain_in):
        copy.start()
    lax.fori_loop(1, group, greet_row, 0)
    lax.fori_loop(1, ny, greet_y, 0)
    lax.fori_loop(1, nx, greet_x, 0)

    row_index = lax.broadcasted_iota(jnp.int32, (LANE, LANE), 0)
    col_index = lax.broadcasted_iota(jnp.int32, (LANE, LANE), 1)
    upper = jnp.where(row_index <= col_index, 1.0, 0.0).astype(F32)
    ld_in.wait()
    cum = jnp.dot(ld[...], upper, precision=HIGHEST, preferred_element_type=F32)
    for h in range(heads):
        spread = jnp.transpose(jnp.broadcast_to(cum[h : h + 1, :], (LANE, LANE)))
        cc[h] = spread
        d_send[h] = jnp.exp(spread[LANE - 1 : LANE, :])

    pl.semaphore_wait(barrier, (group - 1) + (ny - 1) + (nx - 1))

    def send_decay(r, _):
        owner = lax.rem(j + r, group)
        pltpu.make_async_remote_copy(
            src_ref=d_send.at[owner // per_head],
            dst_ref=d_recv.at[j],
            send_sem=d_sem.at[0],
            recv_sem=d_sem.at[1],
            device_id={"ctx": base + owner},
            device_id_type=MESH,
        ).start()
        return 0

    lax.fori_loop(1, group, send_decay, 0)
    d_recv[pl.ds(j, 1)] = d_send[pl.ds(j // per_head, 1)]

    k_in.wait()
    v_in.wait()
    for h in range(heads):
        columns = slice(h * LANE, (h + 1) * LANE)
        spread = cc[h]
        tail = jnp.exp(spread[LANE - 1 : LANE, :] - spread)
        faded = (k[:, columns].astype(F32) * tail).astype(BF16)
        state = lax.dot_general(
            faded, v[:, columns], (((0,), (0,)), ((), ())), preferred_element_type=F32
        )
        s_send[h * per_head : (h + 1) * per_head] = state.astype(BF16).reshape(per_head, rows, LANE)

        def send_slice(owner, _):
            @pl.when(owner != j)
            def _():
                pltpu.make_async_remote_copy(
                    src_ref=s_send.at[owner],
                    dst_ref=z_recv.at[j],
                    send_sem=z_sem.at[0],
                    recv_sem=z_sem.at[1],
                    device_id={"ctx": base + owner},
                    device_id_type=MESH,
                ).start()

            return 0

        lax.fori_loop(h * per_head, (h + 1) * per_head, send_slice, 0)
    z_recv[pl.ds(j, 1)] = s_send[pl.ds(j, 1)]

    def weight_copy(r):
        start = pl.multiple_of(lax.rem(x + r, nx) * width, LANE)
        return pltpu.make_async_copy(w_hbm.at[:, pl.ds(start, width)], w.at[r], w_sem.at[r])

    for step in range(half_x):
        distance = half_x - step
        for r in sorted({distance, nx - distance}):
            weight_copy(r).start()
    weight_copy(0).start()

    def bulk(ref, send_sem, recv_sem):
        return pltpu.make_async_remote_copy(
            src_ref=ref, dst_ref=ref, send_sem=send_sem, recv_sem=recv_sem,
            device_id={"head": lax.rem(x + 1, nx)}, device_id_type=MESH,
        )

    bulk(d_recv.at[pl.ds(0, group - 1)], d_sem.at[0], d_sem.at[1]).wait_recv()
    running = jnp.ones((1, LANE), F32)
    for i in range(group):
        pd_buf[i] = running
        running = running * d_recv[i]
    yd_send[0] = running

    def send_row_decay(r, _):
        pltpu.make_async_remote_copy(
            src_ref=yd_send.at[0],
            dst_ref=yd_recv.at[y],
            send_sem=yd_sem.at[0],
            recv_sem=yd_sem.at[1],
            device_id={"ctx": lax.rem(y + r, ny) * group + j},
            device_id_type=MESH,
        ).start()
        return 0

    if ny > 1:
        lax.fori_loop(1, ny, send_row_decay, 0)

    q_in.wait()
    causal = row_index >= col_index
    for h in range(heads):
        columns = slice(h * LANE, (h + 1) * LANE)
        spread = cc[h]
        scores = lax.dot_general(
            q[:, columns], k[:, columns], (((1,), (1,)), ((), ())), preferred_element_type=F32
        )
        differ = jnp.where(causal, spread - cum[h : h + 1, :], -1e30)
        weights = (jnp.exp(differ) * scores).astype(BF16)
        within[h] = jnp.dot(weights, v[:, columns], preferred_element_type=F32)
        cc[h] = jnp.exp(spread)

    bulk(z_recv.at[pl.ds(0, group - 1)], z_sem.at[0], z_sem.at[1]).wait_recv()
    carry = jnp.zeros((rows, LANE), F32)
    for i in range(group):
        e_buf[i] = carry
        carry = d_recv[i] * carry + z_recv[i].astype(F32)
    r_send[0] = carry.astype(BF16)

    def row_total(target):
        return pltpu.make_async_remote_copy(
            src_ref=r_send.at[0],
            dst_ref=y_recv.at[y],
            send_sem=y_send_sem.at[target],
            recv_sem=y_recv_sem.at[y],
            device_id={"ctx": target * group + j},
            device_id_type=MESH,
        )

    def send_total(target, _):
        row_total(target).start()
        return 0

    lax.fori_loop(y + 1, ny, send_total, 0)
    if ny > 1:
        bulk(yd_recv.at[pl.ds(0, ny - 1)], yd_sem.at[0], yd_sem.at[1]).wait_recv()

    def add_row(i, prefix):
        pltpu.make_async_remote_copy(
            src_ref=y_recv.at[i],
            dst_ref=y_recv.at[i],
            send_sem=y_send_sem.at[i],
            recv_sem=y_recv_sem.at[i],
            device_id={"ctx": i * group + j},
            device_id_type=MESH,
        ).wait_recv()
        return yd_recv[i] * prefix + y_recv[i].astype(F32)

    prefix = lax.fori_loop(0, y, add_row, jnp.zeros((rows, LANE), F32))

    def send_prefix(i, _):
        p_send[i] = (pd_buf[i] * prefix + e_buf[i]).astype(BF16)

        @pl.when(i != j)
        def _():
            pltpu.make_async_remote_copy(
                src_ref=p_send.at[i],
                dst_ref=s_in.at[j],
                send_sem=p_sem.at[0],
                recv_sem=p_sem.at[1],
                device_id={"ctx": base + i},
                device_id_type=MESH,
            ).start()

        return 0

    lax.fori_loop(0, group, send_prefix, 0)
    s_in[pl.ds(j, 1)] = p_send[pl.ds(j, 1)]

    gain_in.wait()
    for step in range(half_x):
        distance = half_x - step
        for r in sorted({distance, nx - distance}):
            weight_copy(r).wait()
    weight_copy(0).wait()

    bulk(s_in.at[pl.ds(0, group - 1)], p_sem.at[0], p_sem.at[1]).wait_recv()
    squares = jnp.zeros((LANE, LANE), F32)
    for h in range(heads):
        columns = slice(h * LANE, (h + 1) * LANE)
        state = s_in[h * per_head : (h + 1) * per_head].reshape(LANE, LANE)
        carried = jnp.dot(q[:, columns], state, preferred_element_type=F32)
        attn = within[h] + cc[h] * carried
        squares = squares + attn * attn
        act[:, columns] = (attn * gain[:, columns]).astype(BF16)

    right, left = lax.rem(x + 1, nx), lax.rem(x + nx - 1, nx)

    def slot(step, c, way):
        if step == 0:
            return c if way == 0 else c - half_c
        return half_c + chunks * (step - 1) + c

    def hop(step, c, way):
        place = slot(step, c, way)
        return pltpu.make_async_remote_copy(
            src_ref=tx.at[way, place],
            dst_ref=rx.at[way, place],
            send_sem=tx_sem.at[way],
            recv_sem=rx_sem.at[way, place],
            device_id={"head": right if way == 0 else left},
            device_id_type=MESH,
        )

    def project(r, pair):
        return jnp.dot(
            act[...], w[r, :, pair * 2 * LANE : (pair + 1) * 2 * LANE], preferred_element_type=F32
        )

    for pair in range(chunks // 2):
        block = project(half_x, pair)
        for c in (2 * pair, 2 * pair + 1):
            way = 0 if c < half_c else 1
            part = block[:, :LANE] if c % 2 == 0 else block[:, LANE:]
            tx[way, slot(0, c, way)] = part.astype(BF16)
            hop(0, c, way).start()

    sq_send[0] = jnp.sum(jnp.transpose(squares), axis=0, keepdims=True)

    def send_squares(r, _):
        pltpu.make_async_remote_copy(
            src_ref=sq_send.at[0],
            dst_ref=sq_recv.at[x],
            send_sem=sq_sem.at[0],
            recv_sem=sq_sem.at[1],
            device_id={"head": lax.rem(x + r, nx)},
            device_id_type=MESH,
        ).start()
        return 0

    lax.fori_loop(1, nx, send_squares, 0)
    sq_recv[pl.ds(x, 1)] = sq_send[...]

    def arrives(step, c, way):
        if step == 0:
            return (c < half_c) == (way == 0)
        return True

    def fill(way, r):
        for pair in range(chunks // 2):
            block = project(r, pair)
            own[way, 2 * pair] = block[:, :LANE]
            own[way, 2 * pair + 1] = block[:, LANE:]

    for step in range(1, half_x):
        distance = half_x - step
        fill(0, distance)
        fill(1, nx - distance)
        order = [list(range(chunks)), list(range(chunks))]
        if step == 1:
            order[0] = order[0][half_c:] + order[0][:half_c]
        for place in range(chunks):
            for way in (0, 1):
                c = order[way][place]
                total = own[way, c]
                if arrives(step - 1, c, way):
                    hop(step - 1, c, way).wait_recv()
                    total = total + rx[way, slot(step - 1, c, way)].astype(F32)
                tx[way, slot(step, c, way)] = total.astype(BF16)
                hop(step, c, way).start()

    fill(0, 0)
    bulk(sq_recv.at[pl.ds(0, nx - 1)], sq_sem.at[0], sq_sem.at[1]).wait_recv()
    total = sq_recv[0]
    for i in range(1, nx):
        total = total + sq_recv[i]
    scale = lax.rsqrt(total / (nx * heads * LANE) + 1e-05)
    scale = jnp.transpose(jnp.broadcast_to(scale, (LANE, LANE)))
    for c in range(chunks):
        block = own[0, c]
        for way in (0, 1):
            if arrives(half_x - 1, c, way):
                hop(half_x - 1, c, way).wait_recv()
                block = block + rx[way, slot(half_x - 1, c, way)].astype(F32)
        out_ref[:, c * LANE : (c + 1) * LANE] = (block * scale).astype(BF16)

    bulk(d_recv.at[pl.ds(0, group - 1)], d_sem.at[0], d_sem.at[1]).wait_send()
    bulk(z_recv.at[pl.ds(0, group - 1)], z_sem.at[0], z_sem.at[1]).wait_send()
    if ny > 1:
        bulk(yd_recv.at[pl.ds(0, ny - 1)], yd_sem.at[0], yd_sem.at[1]).wait_send()
    bulk(s_in.at[pl.ds(0, group - 1)], p_sem.at[0], p_sem.at[1]).wait_send()
    bulk(sq_recv.at[pl.ds(0, nx - 1)], sq_sem.at[0], sq_sem.at[1]).wait_send()

    def left_total(target, _):
        row_total(target).wait_send()
        return 0

    lax.fori_loop(y + 1, ny, left_total, 0)
    for way in (0, 1):
        bulk(tx.at[way], tx_sem.at[way], rx_sem.at[way, 0]).wait_send()


def solution(mesh, group=ROW_GROUP):
    nx, ctx = mesh.shape["head"], mesh.shape["ctx"]
    ny = ctx // group

    def local(query, keys, values, log_decay, norm_gain, out_weight):
        tokens, features = query.shape
        heads = log_decay.shape[1]
        width = out_weight.shape[1] // nx
        chunks = width // LANE
        rows = features // group
        slots = chunks // 2 + chunks * (nx // 2 - 1)
        anywhere = pl.BlockSpec(memory_space=pl.ANY)
        square = (LANE, LANE)
        dma = pltpu.SemaphoreType.DMA
        return pl.pallas_call(
            functools.partial(body, (nx, ny, group, heads, chunks)),
            out_shape=jax.ShapeDtypeStruct((tokens, width), BF16),
            in_specs=[anywhere] * 6,
            out_specs=pl.BlockSpec(memory_space=pltpu.VMEM),
            scratch_shapes=[
                pltpu.VMEM((tokens, features), BF16),
                pltpu.VMEM((tokens, features), BF16),
                pltpu.VMEM((tokens, features), BF16),
                pltpu.VMEM((heads, tokens), F32),
                pltpu.VMEM((1, features), F32),
                pltpu.VMEM((nx, features, width), BF16),
                pltpu.VMEM((heads,) + square, F32),
                pltpu.VMEM((heads,) + square, F32),
                pltpu.VMEM((tokens, features), BF16),
                pltpu.VMEM((heads, 1, LANE), F32),
                pltpu.VMEM((group, 1, LANE), F32),
                pltpu.VMEM((group, rows, LANE), BF16),
                pltpu.VMEM((group, rows, LANE), BF16),
                pltpu.VMEM((group, rows, LANE), F32),
                pltpu.VMEM((group, 1, LANE), F32),
                pltpu.VMEM((1, 1, LANE), F32),
                pltpu.VMEM((ny, 1, LANE), F32),
                pltpu.VMEM((1, rows, LANE), BF16),
                pltpu.VMEM((ny, rows, LANE), BF16),
                pltpu.VMEM((group, rows, LANE), BF16),
                pltpu.VMEM((group, rows, LANE), BF16),
                pltpu.VMEM((1, 1, LANE), F32),
                pltpu.VMEM((nx, 1, LANE), F32),
                pltpu.VMEM((2, chunks) + square, F32),
                pltpu.VMEM((2, slots) + square, BF16),
                pltpu.VMEM((2, slots) + square, BF16),
                dma((5,)),
                dma((nx,)),
                dma((2,)),
                dma((2,)),
                dma((2,)),
                dma((ny,)),
                dma((ny,)),
                dma((2,)),
                dma((2,)),
                dma((2,)),
                dma((2, slots)),
            ],
            compiler_params=pltpu.CompilerParams(
                collective_id=0, has_side_effects=True, vmem_limit_bytes=60 * 2**20
            ),
        )(query, keys, values, log_decay.T, norm_gain.reshape(1, features), out_weight)

    placed = (
        P("ctx", "head"),
        P("ctx", "head"),
        P("ctx", "head"),
        P("ctx", "head"),
        P("head"),
        P("head", None),
    )
    return jax.shard_map(
        local, mesh=mesh, in_specs=placed, out_specs=P("ctx", "head"), check_vma=False
    )
```

time: 493 us -> 57.7 us (0.12)
  the two profiles are of different devices: /device:TPU:2 before, /device:TPU:1 now
where the time goes in v1:
time: 57.7 us; the launch traced here: 57.6 us
  Pallas kernels  55.9 us (97%)
  local copies, waits for them, and re-layouts  1.62 us (3%)
    pallas_call x1, Pallas kernels, local(): pl.pallas_call(functools.partial(body, (nx, ny, group, heads, chunks)), o...  55.9 us
    unnamed x1, local copies, waits for them, and re-layouts  1.62 us

profile of v1, /device:TPU:1, one launch (start us, length us, event | category | flops | bytes accessed | tf_op | source)
XLA Modules:
  0.0 57.6 jit_solution(4203921122632996386)
XLA Ops:
  0.0 55.9 %shard_map.64 = bf16[128,768]{1,0:T(8,128)(2,1)} custom-call(bf16[128,512]{1,0:T(8,128)(2,1)} %q_hbm.1, bf16[128,512]{1,0:T(8,128)(2,1)} %k_hbm.1, bf16[128,512]{1,0:T(8,128)(2,1)} %v_hbm.1, f32[4,128]{1,0:T(4,128)} %bitcast.2, f32[1,512]{1,0:T(1,128)} %bitcast.3, bf16[512,6144]{1,0:T(8,128)(2,1)} %w_hbm.1), custom_call_target="tpu_custom_call" | custom-call | tf_op jit(solution)/shard_map/pallas_call | solution.py:373
  55.9 1.6 %copy.8 = bf16[128,768]{1,0:T(8,128)(2,1)} copy(bf16[128,768]{1,0:T(8,128)(2,1)} %shard_map.64) | data formatting | bytes 393216

commit v2 on v1

--- a/solution.py
+++ b/solution.py
@@ -128,7 +128,7 @@
 
     def weight_copy(r):
         start = pl.multiple_of(lax.rem(x + r, nx) * width, LANE)
-        return pltpu.make_async_copy(w_hbm.at[:, pl.ds(start, width)], w.at[r], w_sem.at[r])
+        return pltpu.make_async_copy(w_hbm.at[:, pl.ds(start, width)], w.at[r], w_sem.at[0])
 
     for step in range(half_x):
         distance = half_x - step
@@ -234,11 +234,7 @@
     s_in[pl.ds(j, 1)] = p_send[pl.ds(j, 1)]
 
     gain_in.wait()
-    for step in range(half_x):
-        distance = half_x - step
-        for r in sorted({distance, nx - distance}):
-            weight_copy(r).wait()
-    weight_copy(0).wait()
+    pltpu.make_async_copy(w, w, w_sem.at[0]).wait()
 
     bulk(s_in.at[pl.ds(0, group - 1)], p_sem.at[0], p_sem.at[1]).wait_recv()
     squares = jnp.zeros((LANE, LANE), F32)
@@ -273,7 +269,7 @@
             act[...], w[r, :, pair * 2 * LANE : (pair + 1) * 2 * LANE], preferred_element_type=F32
         )
 
-    for pair in range(chunks // 2):
+    for pair in sorted(range(chunks // 2), key=lambda p: min(p, chunks // 2 - 1 - p)):
         block = project(half_x, pair)
         for c in (2 * pair, 2 * pair + 1):
             way = 0 if c < half_c else 1
@@ -312,9 +308,7 @@
         distance = half_x - step
         fill(0, distance)
         fill(1, nx - distance)
-        order = [list(range(chunks)), list(range(chunks))]
-        if step == 1:
-            order[0] = order[0][half_c:] + order[0][:half_c]
+        order = [list(range(half_c, chunks)) + list(range(half_c)), list(range(chunks))]
         for place in range(chunks):
             for way in (0, 1):
                 c = order[way][place]
@@ -372,7 +366,7 @@
         dma = pltpu.SemaphoreType.DMA
         return pl.pallas_call(
             functools.partial(body, (nx, ny, group, heads, chunks)),
-            out_shape=jax.ShapeDtypeStruct((tokens, width), BF16),
+            out_shape=pltpu.VMEM((tokens, width), BF16),
             in_specs=[anywhere] * 6,
             out_specs=pl.BlockSpec(memory_space=pltpu.VMEM),
             scratch_shapes=[
@@ -403,7 +397,7 @@
                 pltpu.VMEM((2, slots) + square, BF16),
                 pltpu.VMEM((2, slots) + square, BF16),
                 dma((5,)),
-                dma((nx,)),
+                dma((1,)),
                 dma((2,)),
                 dma((2,)),
                 dma((2,)),

time: 57.7 us -> 55.6 us (0.964)
  Pallas kernels: 55.9 us -> 54.7 us
  local copies, waits for them, and re-layouts: 1.62 us -> 0.68 us
    pallas_call x1, Pallas kernels: 55.9 us -> 54.7 us  [local(): pl.pallas_call(functools.partial(body, (nx, ny, group, heads, chunks)), o...]
    unnamed x1, local copies, waits for them, and re-layouts: 1.62 us -> 0.68 us
where the time goes in v2:
time: 55.6 us; the launch traced here: 55.4 us
  Pallas kernels  54.7 us (98%)
  local copies, waits for them, and re-layouts  0.68 us (1%)
    pallas_call x1, Pallas kernels, local(): pl.pallas_call(functools.partial(body, (nx, ny, group, heads, chunks)), o...  54.7 us

profile of v2, /device:TPU:1, one launch (start us, length us, event | category | flops | bytes accessed | tf_op | source)
XLA Modules:
  0.0 55.4 jit_solution(10059454823130333126)
XLA Ops:
  0.0 54.7 %shard_map.64 = bf16[128,768]{1,0:T(8,128)(2,1)S(1)} custom-call(bf16[128,512]{1,0:T(8,128)(2,1)} %q_hbm.1, bf16[128,512]{1,0:T(8,128)(2,1)} %k_hbm.1, bf16[128,512]{1,0:T(8,128)(2,1)} %v_hbm.1, f32[4,128]{1,0:T(4,128)} %bitcast.2, f32[1,512]{1,0:T(1,128)} %bitcast.3, bf16[512,6144]{1,0:T(8,128)(2,1)} %w_hbm.1), custom_call_target="tpu_custom_call" | custom-call | tf_op jit(solution)/shard_map/pallas_call | solution.py:367
  54.7 0.7 %copy.8 = bf16[128,768]{1,0:T(8,128)(2,1)} copy(bf16[128,768]{1,0:T(8,128)(2,1)S(1)} %shard_map.64) | data formatting | bytes 393216

commit v3 on v2

--- a/solution.py
+++ b/solution.py
@@ -24,7 +24,7 @@
     d_send, d_recv, s_send, z_recv, e_buf, pd_buf,
     yd_send, yd_recv, r_send, y_recv, p_send, s_in,
     sq_send, sq_recv, own, tx, rx,
-    in_sem, w_sem, d_sem, z_sem, yd_sem, y_send_sem, y_recv_sem, p_sem, sq_sem,
+    in_sem, w_sem, d_sem, z_sem, yd_send_sem, yd_recv_sem, y_send_sem, y_recv_sem, p_sem, sq_sem,
     tx_sem, rx_sem,
 ):
     nx, ny, group, heads, chunks = dims
@@ -136,33 +136,6 @@
             weight_copy(r).start()
     weight_copy(0).start()
 
-    def bulk(ref, send_sem, recv_sem):
-        return pltpu.make_async_remote_copy(
-            src_ref=ref, dst_ref=ref, send_sem=send_sem, recv_sem=recv_sem,
-            device_id={"head": lax.rem(x + 1, nx)}, device_id_type=MESH,
-        )
-
-    bulk(d_recv.at[pl.ds(0, group - 1)], d_sem.at[0], d_sem.at[1]).wait_recv()
-    running = jnp.ones((1, LANE), F32)
-    for i in range(group):
-        pd_buf[i] = running
-        running = running * d_recv[i]
-    yd_send[0] = running
-
-    def send_row_decay(r, _):
-        pltpu.make_async_remote_copy(
-            src_ref=yd_send.at[0],
-            dst_ref=yd_recv.at[y],
-            send_sem=yd_sem.at[0],
-            recv_sem=yd_sem.at[1],
-            device_id={"ctx": lax.rem(y + r, ny) * group + j},
-            device_id_type=MESH,
-        ).start()
-        return 0
-
-    if ny > 1:
-        lax.fori_loop(1, ny, send_row_decay, 0)
-
     q_in.wait()
     causal = row_index >= col_index
     for h in range(heads):
@@ -176,6 +149,39 @@
         within[h] = jnp.dot(weights, v[:, columns], preferred_element_type=F32)
         cc[h] = jnp.exp(spread)
 
+    def bulk(ref, send_sem, recv_sem):
+        return pltpu.make_async_remote_copy(
+            src_ref=ref, dst_ref=ref, send_sem=send_sem, recv_sem=recv_sem,
+            device_id={"head": lax.rem(x + 1, nx)}, device_id_type=MESH,
+        )
+
+    bulk(d_recv.at[pl.ds(0, group - 1)], d_sem.at[0], d_sem.at[1]).wait_recv()
+    running = jnp.ones((1, LANE), F32)
+    for i in range(group):
+        pd_buf[i] = running
+        running = running * d_recv[i]
+    yd_send[0] = running
+
+    def row_decay(target):
+        return pltpu.make_async_remote_copy(
+            src_ref=yd_send.at[0],
+            dst_ref=yd_recv.at[y],
+            send_sem=yd_send_sem.at[target],
+            recv_sem=yd_recv_sem.at[y],
+            device_id={"ctx": target * group + j},
+            device_id_type=MESH,
+        )
+
+    offsets = sorted(range(1, ny), key=lambda r: -min(r, ny - r))
+
+    def each_later(act_on):
+        for r in offsets:
+            @pl.when(y + r < ny)
+            def _():
+                act_on(y + r)
+
+    each_later(lambda target: row_decay(target).start())
+
     bulk(z_recv.at[pl.ds(0, group - 1)], z_sem.at[0], z_sem.at[1]).wait_recv()
     carry = jnp.zeros((rows, LANE), F32)
     for i in range(group):
@@ -193,13 +199,7 @@
             device_id_type=MESH,
         )
 
-    def send_total(target, _):
-        row_total(target).start()
-        return 0
-
-    lax.fori_loop(y + 1, ny, send_total, 0)
-    if ny > 1:
-        bulk(yd_recv.at[pl.ds(0, ny - 1)], yd_sem.at[0], yd_sem.at[1]).wait_recv()
+    each_later(lambda target: row_total(target).start())
 
     def add_row(i, prefix):
         pltpu.make_async_remote_copy(
@@ -207,6 +207,14 @@
             dst_ref=y_recv.at[i],
             send_sem=y_send_sem.at[i],
             recv_sem=y_recv_sem.at[i],
+            device_id={"ctx": i * group + j},
+            device_id_type=MESH,
+        ).wait_recv()
+        pltpu.make_async_remote_copy(
+            src_ref=yd_recv.at[i],
+            dst_ref=yd_recv.at[i],
+            send_sem=yd_send_sem.at[i],
+            recv_sem=yd_recv_sem.at[i],
             device_id={"ctx": i * group + j},
             device_id_type=MESH,
         ).wait_recv()
@@ -336,16 +344,14 @@
 
     bulk(d_recv.at[pl.ds(0, group - 1)], d_sem.at[0], d_sem.at[1]).wait_send()
     bulk(z_recv.at[pl.ds(0, group - 1)], z_sem.at[0], z_sem.at[1]).wait_send()
-    if ny > 1:
-        bulk(yd_recv.at[pl.ds(0, ny - 1)], yd_sem.at[0], yd_sem.at[1]).wait_send()
     bulk(s_in.at[pl.ds(0, group - 1)], p_sem.at[0], p_sem.at[1]).wait_send()
     bulk(sq_recv.at[pl.ds(0, nx - 1)], sq_sem.at[0], sq_sem.at[1]).wait_send()
 
-    def left_total(target, _):
+    def departed(target):
         row_total(target).wait_send()
-        return 0
-
-    lax.fori_loop(y + 1, ny, left_total, 0)
+        row_decay(target).wait_send()
+
+    each_later(departed)
     for way in (0, 1):
         bulk(tx.at[way], tx_sem.at[way], rx_sem.at[way, 0]).wait_send()
 
@@ -400,7 +406,8 @@
                 dma((1,)),
                 dma((2,)),
                 dma((2,)),
-                dma((2,)),
+                dma((ny,)),
+                dma((ny,)),
                 dma((ny,)),
                 dma((ny,)),
                 dma((2,)),

time: 55.6 us -> 54.1 us (0.973)
  the two profiles are of different devices: /device:TPU:1 before, /device:TPU:114 now
where the time goes in v3:
time: 54.1 us; the launch traced here: 54 us
  Pallas kernels  53.3 us (99%)
  local copies, waits for them, and re-layouts  0.68 us (1%)
    pallas_call x1, Pallas kernels, local(): pl.pallas_call(functools.partial(body, (nx, ny, group, heads, chunks)), o...  53.3 us

profile of v3, /device:TPU:114, one launch (start us, length us, event | category | flops | bytes accessed | tf_op | source)
XLA Modules:
  0.0 54.0 jit_solution(3391151659304106130)
XLA Ops:
  0.0 53.3 %shard_map.64 = bf16[128,768]{1,0:T(8,128)(2,1)S(1)} custom-call(bf16[128,512]{1,0:T(8,128)(2,1)} %q_hbm.1, bf16[128,512]{1,0:T(8,128)(2,1)} %k_hbm.1, bf16[128,512]{1,0:T(8,128)(2,1)} %v_hbm.1, f32[4,128]{1,0:T(4,128)} %bitcast.2, f32[1,512]{1,0:T(1,128)} %bitcast.3, bf16[512,6144]{1,0:T(8,128)(2,1)} %w_hbm.1), custom_call_target="tpu_custom_call" | custom-call | tf_op jit(solution)/shard_map/pallas_call | solution.py:373
  53.3 0.7 %copy.8 = bf16[128,768]{1,0:T(8,128)(2,1)} copy(bf16[128,768]{1,0:T(8,128)(2,1)S(1)} %shard_map.64) | data formatting | bytes 393216

commit v4 on v3

--- a/solution.py
+++ b/solution.py
@@ -24,7 +24,7 @@
     d_send, d_recv, s_send, z_recv, e_buf, pd_buf,
     yd_send, yd_recv, r_send, y_recv, p_send, s_in,
     sq_send, sq_recv, own, tx, rx,
-    in_sem, w_sem, d_sem, z_sem, yd_send_sem, yd_recv_sem, y_send_sem, y_recv_sem, p_sem, sq_sem,
+    in_sem, w_sem, d_sem, z_sem, sent_sem, yd_send_sem, yd_recv_sem, y_send_sem, y_recv_sem, p_sem, sq_sem,
     tx_sem, rx_sem,
 ):
     nx, ny, group, heads, chunks = dims
@@ -38,6 +38,28 @@
     half_c = chunks // 2
     width = chunks * LANE
     per_head = LANE // rows
+    slices = heads * per_head
+    nz = group // 2
+
+    z_at, core = j // 2, lax.rem(j, 2)
+    far = z_at // (nz // 2)
+    rank = far * (z_at - (nz - 3)) + (1 - far) * (2 - z_at)
+
+    def owner_of(s):
+        level, near = min(s // 4, 2), (s // 2) % 2
+        z_owner = 2 - level if near else nz - 3 + level
+        return 2 * z_owner + s % 2, s // 4 - level
+
+    def slice_of(slot):
+        return 4 * (rank + slot) + 2 * (1 - far) + core
+
+    def owning(slot, act_on):
+        pl.when(rank >= 2 * slot)(functools.partial(act_on, slot))
+
+    def exchanged(act_on):
+        pl.when(rank == 2)(functools.partial(act_on, slices - 2))
+        pl.when((rank >= 0) & (rank < 2))(functools.partial(act_on, slices - 1))
+        pl.when(rank < 0)(functools.partial(act_on, slices))
 
     barrier = pltpu.get_barrier_semaphore()
 
@@ -82,20 +104,28 @@
 
     pl.semaphore_wait(barrier, (group - 1) + (ny - 1) + (nx - 1))
 
-    def send_decay(r, _):
-        owner = lax.rem(j + r, group)
-        pltpu.make_async_remote_copy(
-            src_ref=d_send.at[owner // per_head],
-            dst_ref=d_recv.at[j],
-            send_sem=d_sem.at[0],
-            recv_sem=d_sem.at[1],
-            device_id={"ctx": base + owner},
-            device_id_type=MESH,
-        ).start()
-        return 0
-
-    lax.fori_loop(1, group, send_decay, 0)
-    d_recv[pl.ds(j, 1)] = d_send[pl.ds(j // per_head, 1)]
+    def to_owner(s, src, dst, send_sem, recv_sem):
+        owner, slot = owner_of(s)
+
+        @pl.when(owner != j)
+        def _():
+            pltpu.make_async_remote_copy(
+                src_ref=src,
+                dst_ref=dst.at[slot, j],
+                send_sem=send_sem,
+                recv_sem=recv_sem.at[slot],
+                device_id={"ctx": base + owner},
+                device_id_type=MESH,
+            ).start()
+
+    for s in range(slices):
+        to_owner(s, d_send.at[s // per_head], d_recv, sent_sem.at[0], d_sem)
+
+    def keep_decay(slot):
+        d_recv[slot, pl.ds(j, 1)] = d_send[pl.ds(slice_of(slot) // per_head, 1)]
+
+    owning(0, keep_decay)
+    owning(1, keep_decay)
 
     k_in.wait()
     v_in.wait()
@@ -109,22 +139,14 @@
         )
         s_send[h * per_head : (h + 1) * per_head] = state.astype(BF16).reshape(per_head, rows, LANE)
 
-        def send_slice(owner, _):
-            @pl.when(owner != j)
-            def _():
-                pltpu.make_async_remote_copy(
-                    src_ref=s_send.at[owner],
-                    dst_ref=z_recv.at[j],
-                    send_sem=z_sem.at[0],
-                    recv_sem=z_sem.at[1],
-                    device_id={"ctx": base + owner},
-                    device_id_type=MESH,
-                ).start()
-
-            return 0
-
-        lax.fori_loop(h * per_head, (h + 1) * per_head, send_slice, 0)
-    z_recv[pl.ds(j, 1)] = s_send[pl.ds(j, 1)]
+        for s in range(h * per_head, (h + 1) * per_head):
+            to_owner(s, s_send.at[s], z_recv, sent_sem.at[1], z_sem)
+
+    def keep_slice(slot):
+        z_recv[slot, pl.ds(j, 1)] = s_send[pl.ds(slice_of(slot), 1)]
+
+    owning(0, keep_slice)
+    owning(1, keep_slice)
 
     def weight_copy(r):
         start = pl.multiple_of(lax.rem(x + r, nx) * width, LANE)
@@ -155,19 +177,22 @@
             device_id={"head": lax.rem(x + 1, nx)}, device_id_type=MESH,
         )
 
-    bulk(d_recv.at[pl.ds(0, group - 1)], d_sem.at[0], d_sem.at[1]).wait_recv()
-    running = jnp.ones((1, LANE), F32)
-    for i in range(group):
-        pd_buf[i] = running
-        running = running * d_recv[i]
-    yd_send[0] = running
-
-    def row_decay(target):
+    def row_decay(slot, target):
         return pltpu.make_async_remote_copy(
-            src_ref=yd_send.at[0],
-            dst_ref=yd_recv.at[y],
-            send_sem=yd_send_sem.at[target],
-            recv_sem=yd_recv_sem.at[y],
+            src_ref=yd_send.at[slot],
+            dst_ref=yd_recv.at[slot, y],
+            send_sem=yd_send_sem.at[slot, target],
+            recv_sem=yd_recv_sem.at[slot, y],
+            device_id={"ctx": target * group + j},
+            device_id_type=MESH,
+        )
+
+    def row_total(slot, target):
+        return pltpu.make_async_remote_copy(
+            src_ref=r_send.at[slot],
+            dst_ref=y_recv.at[slot, y],
+            send_sem=y_send_sem.at[slot, target],
+            recv_sem=y_recv_sem.at[slot, y],
             device_id={"ctx": target * group + j},
             device_id_type=MESH,
         )
@@ -180,71 +205,62 @@
             def _():
                 act_on(y + r)
 
-    each_later(lambda target: row_decay(target).start())
-
-    bulk(z_recv.at[pl.ds(0, group - 1)], z_sem.at[0], z_sem.at[1]).wait_recv()
-    carry = jnp.zeros((rows, LANE), F32)
-    for i in range(group):
-        e_buf[i] = carry
-        carry = d_recv[i] * carry + z_recv[i].astype(F32)
-    r_send[0] = carry.astype(BF16)
-
-    def row_total(target):
-        return pltpu.make_async_remote_copy(
-            src_ref=r_send.at[0],
-            dst_ref=y_recv.at[y],
-            send_sem=y_send_sem.at[target],
-            recv_sem=y_recv_sem.at[y],
-            device_id={"ctx": target * group + j},
-            device_id_type=MESH,
-        )
-
-    each_later(lambda target: row_total(target).start())
-
-    def add_row(i, prefix):
-        pltpu.make_async_remote_copy(
-            src_ref=y_recv.at[i],
-            dst_ref=y_recv.at[i],
-            send_sem=y_send_sem.at[i],
-            recv_sem=y_recv_sem.at[i],
-            device_id={"ctx": i * group + j},
-            device_id_type=MESH,
-        ).wait_recv()
-        pltpu.make_async_remote_copy(
-            src_ref=yd_recv.at[i],
-            dst_ref=yd_recv.at[i],
-            send_sem=yd_send_sem.at[i],
-            recv_sem=yd_recv_sem.at[i],
-            device_id={"ctx": i * group + j},
-            device_id_type=MESH,
-        ).wait_recv()
-        return yd_recv[i] * prefix + y_recv[i].astype(F32)
-
-    prefix = lax.fori_loop(0, y, add_row, jnp.zeros((rows, LANE), F32))
-
-    def send_prefix(i, _):
-        p_send[i] = (pd_buf[i] * prefix + e_buf[i]).astype(BF16)
-
-        @pl.when(i != j)
-        def _():
-            pltpu.make_async_remote_copy(
-                src_ref=p_send.at[i],
-                dst_ref=s_in.at[j],
-                send_sem=p_sem.at[0],
-                recv_sem=p_sem.at[1],
-                device_id={"ctx": base + i},
-                device_id_type=MESH,
-            ).start()
-
-        return 0
-
-    lax.fori_loop(0, group, send_prefix, 0)
-    s_in[pl.ds(j, 1)] = p_send[pl.ds(j, 1)]
+    def fold_decays(slot):
+        bulk(d_recv.at[slot, pl.ds(0, group - 1)], sent_sem.at[0], d_sem.at[slot]).wait_recv()
+        running = jnp.ones((1, LANE), F32)
+        for i in range(group):
+            pd_buf[slot, i] = running
+            running = running * d_recv[slot, i]
+        yd_send[slot] = running
+        each_later(lambda target: row_decay(slot, target).start())
+
+    def scan_row(slot):
+        bulk(z_recv.at[slot, pl.ds(0, group - 1)], sent_sem.at[1], z_sem.at[slot]).wait_recv()
+        carry = jnp.zeros((rows, LANE), F32)
+        for i in range(group):
+            e_buf[slot, i] = carry
+            carry = d_recv[slot, i] * carry + z_recv[slot, i].astype(F32)
+        r_send[slot] = carry.astype(BF16)
+        each_later(lambda target: row_total(slot, target).start())
+
+    def prefixes(slot):
+        def add_row(i, prefix):
+            for ref, send_sem, recv_sem in (
+                (y_recv, y_send_sem, y_recv_sem), (yd_recv, yd_send_sem, yd_recv_sem)
+            ):
+                bulk(ref.at[slot, i], send_sem.at[slot, i], recv_sem.at[slot, i]).wait_recv()
+            return yd_recv[slot, i] * prefix + y_recv[slot, i].astype(F32)
+
+        prefix = lax.fori_loop(0, y, add_row, jnp.zeros((rows, LANE), F32))
+        mine = slice_of(slot)
+
+        def send_prefix(i, _):
+            p_send[slot, i] = (pd_buf[slot, i] * prefix + e_buf[slot, i]).astype(BF16)
+
+            @pl.when(i != j)
+            def _():
+                pltpu.make_async_remote_copy(
+                    src_ref=p_send.at[slot, i],
+                    dst_ref=s_in.at[mine],
+                    send_sem=sent_sem.at[2 + slot],
+                    recv_sem=p_sem.at[0],
+                    device_id={"ctx": base + i},
+                    device_id_type=MESH,
+                ).start()
+
+            return 0
+
+        lax.fori_loop(0, group, send_prefix, 0)
+        s_in[pl.ds(mine, 1)] = p_send[slot, pl.ds(j, 1)]
+
+    for stage in (fold_decays, scan_row, prefixes):
+        owning(0, stage)
+        owning(1, stage)
 
     gain_in.wait()
     pltpu.make_async_copy(w, w, w_sem.at[0]).wait()
 
-    bulk(s_in.at[pl.ds(0, group - 1)], p_sem.at[0], p_sem.at[1]).wait_recv()
+    exchanged(lambda count: bulk(s_in.at[pl.ds(0, count)], sent_sem.at[2], p_sem.at[0]).wait_recv())
     squares = jnp.zeros((LANE, LANE), F32)
     for h in range(heads):
         columns = slice(h * LANE, (h + 1) * LANE)
@@ -342,16 +358,24 @@
                 block = block + rx[way, slot(half_x - 1, c, way)].astype(F32)
         out_ref[:, c * LANE : (c + 1) * LANE] = (block * scale).astype(BF16)
 
-    bulk(d_recv.at[pl.ds(0, group - 1)], d_sem.at[0], d_sem.at[1]).wait_send()
-    bulk(z_recv.at[pl.ds(0, group - 1)], z_sem.at[0], z_sem.at[1]).wait_send()
-    bulk(s_in.at[pl.ds(0, group - 1)], p_sem.at[0], p_sem.at[1]).wait_send()
+    def slices_left(count):
+        bulk(pd_buf.at[0, pl.ds(0, count)], sent_sem.at[0], d_sem.at[0]).wait_send()
+        bulk(s_send.at[pl.ds(0, count)], sent_sem.at[1], z_sem.at[0]).wait_send()
+
+    exchanged(slices_left)
+
+    def owner_left(slot):
+        bulk(p_send.at[slot, pl.ds(0, group - 1)], sent_sem.at[2 + slot], p_sem.at[0]).wait_send()
+
+        def departed(target):
+            row_total(slot, target).wait_send()
+            row_decay(slot, target).wait_send()
+
+        each_later(departed)
+
+    owning(0, owner_left)
+    owning(1, owner_left)
     bulk(sq_recv.at[pl.ds(0, nx - 1)], sq_sem.at[0], sq_sem.at[1]).wait_send()
-
-    def departed(target):
-        row_total(target).wait_send()
-        row_decay(target).wait_send()
-
-    each_later(departed)
     for way in (0, 1):
         bulk(tx.at[way], tx_sem.at[way], rx_sem.at[way, 0]).wait_send()
 
@@ -365,7 +389,7 @@
         heads = log_decay.shape[1]
         width = out_weight.shape[1] // nx
         chunks = width // LANE
-        rows = features // group
+        rows = features // 16
         slots = chunks // 2 + chunks * (nx // 2 - 1)
         anywhere = pl.BlockSpec(memory_space=pl.ANY)
         square = (LANE, LANE)
@@ -386,17 +410,17 @@
                 pltpu.VMEM((heads,) + square, F32),
                 pltpu.VMEM((tokens, features), BF16),
                 pltpu.VMEM((heads, 1, LANE), F32),
-                pltpu.VMEM((group, 1, LANE), F32),
-                pltpu.VMEM((group, rows, LANE), BF16),
-                pltpu.VMEM((group, rows, LANE), BF16),
-                pltpu.VMEM((group, rows, LANE), F32),
-                pltpu.VMEM((group, 1, LANE), F32),
-                pltpu.VMEM((1, 1, LANE), F32),
-                pltpu.VMEM((ny, 1, LANE), F32),
-                pltpu.VMEM((1, rows, LANE), BF16),
-                pltpu.VMEM((ny, rows, LANE), BF16),
-                pltpu.VMEM((group, rows, LANE), BF16),
-                pltpu.VMEM((group, rows, LANE), BF16),
+                pltpu.VMEM((2, group, 1, LANE), F32),
+                pltpu.VMEM((16, rows, LANE), BF16),
+                pltpu.VMEM((2, group, rows, LANE), BF16),
+                pltpu.VMEM((2, group, rows, LANE), F32),
+                pltpu.VMEM((2, group, 1, LANE), F32),
+                pltpu.VMEM((2, 1, LANE), F32),
+                pltpu.VMEM((2, ny, 1, LANE), F32),
+                pltpu.VMEM((2, rows, LANE), BF16),
+                pltpu.VMEM((2, ny, rows, LANE), BF16),
+                pltpu.VMEM((2, group, rows, LANE), BF16),
+                pltpu.VMEM((16, rows, LANE), BF16),
                 pltpu.VMEM((1, 1, LANE), F32),
                 pltpu.VMEM((nx, 1, LANE), F32),
                 pltpu.VMEM((2, chunks) + square, F32),
@@ -406,11 +430,12 @@
                 dma((1,)),
                 dma((2,)),
                 dma((2,)),
-                dma((ny,)),
-                dma((ny,)),
-                dma((ny,)),
-                dma((ny,)),
-                dma((2,)),
+                dma((4,)),
+                dma((2, ny)),
+                dma((2, ny)),
+                dma((2, ny)),
+                dma((2, ny)),
+                dma((1,)),
                 dma((2,)),
                 dma((2,)),
                 dma((2, slots)),

time: 54.1 us -> 54.5 us (level)
  no operation moved by 1% of the time
where the time goes in v4:
time: 54.5 us; the launch traced here: 54.4 us
  Pallas kernels  53.7 us (99%)
  local copies, waits for them, and re-layouts  0.68 us (1%)
    pallas_call x1, Pallas kernels, local(): pl.pallas_call(functools.partial(body, (nx, ny, group, heads, chunks)), o...  53.7 us

profile of v4, /device:TPU:114, one launch (start us, length us, event | category | flops | bytes accessed | tf_op | source)
XLA Modules:
  0.0 54.4 jit_solution(5767257411604300516)
XLA Ops:
  0.0 53.7 %shard_map.64 = bf16[128,768]{1,0:T(8,128)(2,1)S(1)} custom-call(bf16[128,512]{1,0:T(8,128)(2,1)} %q_hbm.1, bf16[128,512]{1,0:T(8,128)(2,1)} %k_hbm.1, bf16[128,512]{1,0:T(8,128)(2,1)} %v_hbm.1, f32[4,128]{1,0:T(4,128)} %bitcast.2, f32[1,512]{1,0:T(1,128)} %bitcast.3, bf16[512,6144]{1,0:T(8,128)(2,1)} %w_hbm.1), custom_call_target="tpu_custom_call" | custom-call | tf_op jit(solution)/shard_map/pallas_call | solution.py:397
  53.7 0.7 %copy.8 = bf16[128,768]{1,0:T(8,128)(2,1)} copy(bf16[128,768]{1,0:T(8,128)(2,1)S(1)} %shard_map.64) | data formatting | bytes 393216

commit v5 on v3

--- a/solution.py
+++ b/solution.py
@@ -66,9 +66,12 @@
     gain_in = pltpu.make_async_copy(gain_hbm, gain, in_sem.at[4])
     for copy in (ld_in, k_in, v_in, q_in, gain_in):
         copy.start()
+    offsets = sorted(range(1, ny), key=lambda r: -min(r, ny - r))
+    for r in offsets:
+        greet_y(r, 0)
+    for r in sorted(range(1, nx), key=lambda r: -min(r, nx - r)):
+        greet_x(r, 0)
     lax.fori_loop(1, group, greet_row, 0)
-    lax.fori_loop(1, ny, greet_y, 0)
-    lax.fori_loop(1, nx, greet_x, 0)
 
     row_index = lax.broadcasted_iota(jnp.int32, (LANE, LANE), 0)
     col_index = lax.broadcasted_iota(jnp.int32, (LANE, LANE), 1)
@@ -80,23 +83,6 @@
         cc[h] = spread
         d_send[h] = jnp.exp(spread[LANE - 1 : LANE, :])
 
-    pl.semaphore_wait(barrier, (group - 1) + (ny - 1) + (nx - 1))
-
-    def send_decay(r, _):
-        owner = lax.rem(j + r, group)
-        pltpu.make_async_remote_copy(
-            src_ref=d_send.at[owner // per_head],
-            dst_ref=d_recv.at[j],
-            send_sem=d_sem.at[0],
-            recv_sem=d_sem.at[1],
-            device_id={"ctx": base + owner},
-            device_id_type=MESH,
-        ).start()
-        return 0
-
-    lax.fori_loop(1, group, send_decay, 0)
-    d_recv[pl.ds(j, 1)] = d_send[pl.ds(j // per_head, 1)]
-
     k_in.wait()
     v_in.wait()
     for h in range(heads):
@@ -109,21 +95,22 @@
         )
         s_send[h * per_head : (h + 1) * per_head] = state.astype(BF16).reshape(per_head, rows, LANE)
 
-        def send_slice(owner, _):
-            @pl.when(owner != j)
-            def _():
-                pltpu.make_async_remote_copy(
-                    src_ref=s_send.at[owner],
-                    dst_ref=z_recv.at[j],
-                    send_sem=z_sem.at[0],
-                    recv_sem=z_sem.at[1],
-                    device_id={"ctx": base + owner},
-                    device_id_type=MESH,
-                ).start()
-
-            return 0
-
-        lax.fori_loop(h * per_head, (h + 1) * per_head, send_slice, 0)
+    pl.semaphore_wait(barrier, (group - 1) + (ny - 1) + (nx - 1))
+
+    for r in sorted(range(1, group), key=lambda r: -min(r, group - r)):
+        owner = lax.rem(j + r, group)
+        for src, dst, sem in (
+            (d_send.at[owner // per_head], d_recv, d_sem), (s_send.at[owner], z_recv, z_sem)
+        ):
+            pltpu.make_async_remote_copy(
+                src_ref=src,
+                dst_ref=dst.at[j],
+                send_sem=sem.at[0],
+                recv_sem=sem.at[1],
+                device_id={"ctx": base + owner},
+                device_id_type=MESH,
+            ).start()
+    d_recv[pl.ds(j, 1)] = d_send[pl.ds(j // per_head, 1)]
     z_recv[pl.ds(j, 1)] = s_send[pl.ds(j, 1)]
 
     def weight_copy(r):
@@ -171,8 +158,6 @@
             device_id={"ctx": target * group + j},
             device_id_type=MESH,
         )
-
-    offsets = sorted(range(1, ny), key=lambda r: -min(r, ny - r))
 
     def each_later(act_on):
         for r in offsets:

time: 54.1 us -> 53.4 us (0.987)
  Pallas kernels: 53.3 us -> 52.6 us
    pallas_call x1, Pallas kernels: 53.3 us -> 52.6 us  [local(): pl.pallas_call(functools.partial(body, (nx, ny, group, heads, chunks)), o...]
where the time goes in v5:
time: 53.4 us; the launch traced here: 53.3 us
  Pallas kernels  52.6 us (99%)
  local copies, waits for them, and re-layouts  0.68 us (1%)
    pallas_call x1, Pallas kernels, local(): pl.pallas_call(functools.partial(body, (nx, ny, group, heads, chunks)), o...  52.6 us

profile of v5, /device:TPU:114, one launch (start us, length us, event | category | flops | bytes accessed | tf_op | source)
XLA Modules:
  0.0 53.3 jit_solution(15341131357054845706)
XLA Ops:
  0.0 52.6 %shard_map.64 = bf16[128,768]{1,0:T(8,128)(2,1)S(1)} custom-call(bf16[128,512]{1,0:T(8,128)(2,1)} %q_hbm.1, bf16[128,512]{1,0:T(8,128)(2,1)} %k_hbm.1, bf16[128,512]{1,0:T(8,128)(2,1)} %v_hbm.1, f32[4,128]{1,0:T(4,128)} %bitcast.2, f32[1,512]{1,0:T(1,128)} %bitcast.3, bf16[512,6144]{1,0:T(8,128)(2,1)} %w_hbm.1), custom_call_target="tpu_custom_call" | custom-call | tf_op jit(solution)/shard_map/pallas_call | solution.py:358
  52.6 0.7 %copy.8 = bf16[128,768]{1,0:T(8,128)(2,1)} copy(bf16[128,768]{1,0:T(8,128)(2,1)S(1)} %shard_map.64) | data formatting | bytes 393216

commit v6 on v5

--- a/solution.py
+++ b/solution.py
@@ -291,28 +291,35 @@
             return (c < half_c) == (way == 0)
         return True
 
-    def fill(way, r):
+    def fill(step, way, r):
         for pair in range(chunks // 2):
             block = project(r, pair)
-            own[way, 2 * pair] = block[:, :LANE]
-            own[way, 2 * pair + 1] = block[:, LANE:]
-
+            own[2 * step + way, 2 * pair] = block[:, :LANE]
+            own[2 * step + way, 2 * pair + 1] = block[:, LANE:]
+
+    def forward(step, c, way):
+        total = own[2 * step + way, c]
+        if arrives(step - 1, c, way):
+            hop(step - 1, c, way).wait_recv()
+            total = total + rx[way, slot(step - 1, c, way)].astype(F32)
+        tx[way, slot(step, c, way)] = total.astype(BF16)
+        hop(step, c, way).start()
+
+    order = [list(range(half_c, chunks)) + list(range(half_c)), list(range(chunks))]
     for step in range(1, half_x):
         distance = half_x - step
-        fill(0, distance)
-        fill(1, nx - distance)
-        order = [list(range(half_c, chunks)) + list(range(half_c)), list(range(chunks))]
-        for place in range(chunks):
+        fill(step, 0, distance)
+        fill(step, 1, nx - distance)
+        if step == 1:
+            for place in range(half_c):
+                for way in (0, 1):
+                    forward(1, order[way][place], way)
+    fill(0, 0, 0)
+    for step in range(1, half_x):
+        for place in range(half_c if step == 1 else 0, chunks):
             for way in (0, 1):
-                c = order[way][place]
-                total = own[way, c]
-                if arrives(step - 1, c, way):
-                    hop(step - 1, c, way).wait_recv()
-                    total = total + rx[way, slot(step - 1, c, way)].astype(F32)
-                tx[way, slot(step, c, way)] = total.astype(BF16)
-                hop(step, c, way).start()
-
-    fill(0, 0)
+                forward(step, order[way][place], way)
+
     bulk(sq_recv.at[pl.ds(0, nx - 1)], sq_sem.at[0], sq_sem.at[1]).wait_recv()
     total = sq_recv[0]
     for i in range(1, nx):
@@ -384,7 +391,7 @@
                 pltpu.VMEM((group, rows, LANE), BF16),
                 pltpu.VMEM((1, 1, LANE), F32),
                 pltpu.VMEM((nx, 1, LANE), F32),
-                pltpu.VMEM((2, chunks) + square, F32),
+                pltpu.VMEM((nx, chunks) + square, F32),
                 pltpu.VMEM((2, slots) + square, BF16),
                 pltpu.VMEM((2, slots) + square, BF16),
                 dma((5,)),

time: 53.4 us -> 53.4 us (level)
  no operation moved by 1% of the time
where the time goes in v6:
time: 53.4 us; the launch traced here: 53.3 us
  Pallas kernels  52.6 us (99%)
  local copies, waits for them, and re-layouts  0.68 us (1%)
    pallas_call x1, Pallas kernels, local(): pl.pallas_call(functools.partial(body, (nx, ny, group, heads, chunks)), o...  52.6 us

profile of v6, /device:TPU:114, one launch (start us, length us, event | category | flops | bytes accessed | tf_op | source)
XLA Modules:
  0.0 53.3 jit_solution(12806102198743410890)
XLA Ops:
  0.0 52.6 %shard_map.64 = bf16[128,768]{1,0:T(8,128)(2,1)S(1)} custom-call(bf16[128,512]{1,0:T(8,128)(2,1)} %q_hbm.1, bf16[128,512]{1,0:T(8,128)(2,1)} %k_hbm.1, bf16[128,512]{1,0:T(8,128)(2,1)} %v_hbm.1, f32[4,128]{1,0:T(4,128)} %bitcast.2, f32[1,512]{1,0:T(1,128)} %bitcast.3, bf16[512,6144]{1,0:T(8,128)(2,1)} %w_hbm.1), custom_call_target="tpu_custom_call" | custom-call | tf_op jit(solution)/shard_map/pallas_call | solution.py:365
  52.6 0.7 %copy.8 = bf16[128,768]{1,0:T(8,128)(2,1)} copy(bf16[128,768]{1,0:T(8,128)(2,1)S(1)} %shard_map.64) | data formatting | bytes 393216

commit v7 on v6

--- a/solution.py
+++ b/solution.py
@@ -207,10 +207,10 @@
 
     prefix = lax.fori_loop(0, y, add_row, jnp.zeros((rows, LANE), F32))
 
-    def send_prefix(i, _):
+    for i in range(group):
         p_send[i] = (pd_buf[i] * prefix + e_buf[i]).astype(BF16)
 
-        @pl.when(i != j)
+        @pl.when(j != i)
         def _():
             pltpu.make_async_remote_copy(
                 src_ref=p_send.at[i],
@@ -221,9 +221,6 @@
                 device_id_type=MESH,
             ).start()
 
-        return 0
-
-    lax.fori_loop(0, group, send_prefix, 0)
     s_in[pl.ds(j, 1)] = p_send[pl.ds(j, 1)]
 
     gain_in.wait()

time: 53.4 us -> 53.4 us (level)
  no operation moved by 1% of the time
where the time goes in v7:
time: 53.4 us; the launch traced here: 53.3 us
  Pallas kernels  52.6 us (99%)
  local copies, waits for them, and re-layouts  0.68 us (1%)
    pallas_call x1, Pallas kernels, local(): pl.pallas_call(functools.partial(body, (nx, ny, group, heads, chunks)), o...  52.6 us

profile of v7, /device:TPU:114, one launch (start us, length us, event | category | flops | bytes accessed | tf_op | source)
XLA Modules:
  0.0 53.3 jit_solution(16112871361193447903)
XLA Ops:
  0.0 52.6 %shard_map.64 = bf16[128,768]{1,0:T(8,128)(2,1)S(1)} custom-call(bf16[128,512]{1,0:T(8,128)(2,1)} %q_hbm.1, bf16[128,512]{1,0:T(8,128)(2,1)} %k_hbm.1, bf16[128,512]{1,0:T(8,128)(2,1)} %v_hbm.1, f32[4,128]{1,0:T(4,128)} %bitcast.2, f32[1,512]{1,0:T(1,128)} %bitcast.3, bf16[512,6144]{1,0:T(8,128)(2,1)} %w_hbm.1), custom_call_target="tpu_custom_call" | custom-call | tf_op jit(solution)/shard_map/pallas_call | solution.py:362
  52.6 0.7 %copy.8 = bf16[128,768]{1,0:T(8,128)(2,1)} copy(bf16[128,768]{1,0:T(8,128)(2,1)S(1)} %shard_map.64) | data formatting | bytes 393216
